TPU v7x, 128 devices: a whole 4x4x4 slice. The times are simulated.
128 devices in a mesh: row: 8 (over x, core), col: 16 (over y, z).
Axes of the slice: x: 4, y: 4, z: 4, core: 2. Of those that a mesh axis runs over, the one named last changes fastest.
Arguments:
- density_factor: bfloat16 [524288, 256], P(('row', 'col'))
- onsite: float32 [524288], P(('row', 'col')), may hold values from -4 to 4
- neighbour_ids: int32 [1024, 8], P(('row', 'col')), may hold values from 0 to 1023, as said below
- neighbour_count: int32 [1024], P(('row', 'col')), may hold values from 1 to 8, as said below
- coupling_type: int32 [1024, 8], P(('row', 'col')), may hold values from 0 to 3
- coupling_blocks: bfloat16 [4, 512, 512], replicated, may hold values from -0.25 to 0.25
- bath_pattern: int32 [1024], P(('row', 'col')), may hold values from 0 to 3
- bath_blocks: bfloat16 [4, 512, 512], replicated, may hold values from -0.25 to 0.25
Outputs:
- new_factor: bfloat16 [524288, 256], P(('row', 'col'))
Inputs may be any that keep to these rules, and one draw needn't show every extreme that they name: `neighbour_ids`: every neighbour of block b lies among the 128 blocks that share b's index of row, at most half of 128 blocks from b when that group is taken as a loop, and is never b itself; some block has a neighbour exactly half of 128 blocks away. Only the first neighbour_count[b] slots of block b's lists are used; some block uses all 8.
All inputs are finite; a program needn't handle non-finite values.
Results may differ from a plain program's by a relative error of at most 0.0056.
Values may be sent and summed in bfloat16 or wider, within the bound.
A program may use at most 192 MiB of HBM per device.

v0:
```python
import jax
import jax.numpy as jnp
from jax import lax
from jax.sharding import PartitionSpec as P

SWEEPS = 2
time_step = 0.25


def orthonormal_steps(gram, rank_cols):
    basis = jnp.eye(2 * rank_cols, rank_cols, dtype=jnp.float32)
    for sweep in range(SWEEPS):
        image = jnp.dot(gram, basis, precision=lax.Precision.HIGHEST)
        inner = jnp.dot(image.T, image, precision=lax.Precision.HIGHEST)
        factor = jnp.linalg.cholesky(inner)
        basis = lax.linalg.triangular_solve(
            factor, image, left_side=False, lower=True, transpose_a=True
        )
    return basis


def shards(
    density_factor,
    onsite,
    neighbour_ids,
    neighbour_count,
    coupling_type,
    coupling_blocks,
    bath_pattern,
    bath_blocks,
):
    blocks, slots = neighbour_ids.shape
    kinds = coupling_blocks.shape[0]
    block_rows = coupling_blocks.shape[1]
    rank_cols = density_factor.shape[1]
    col_count = lax.axis_size("col")
    group_blocks = col_count * blocks
    row_place = lax.axis_index("row")
    in_group = neighbour_ids - row_place * group_blocks
    slot_live = jnp.arange(slots, dtype=jnp.int32)[None, :] < neighbour_count[:, None]
    kind_match = (
        coupling_type[:, :, None] == jnp.arange(kinds, dtype=jnp.int32)[None, None, :]
    ) & slot_live[:, :, None]
    kind_float = kind_match.astype(jnp.float32)
    gathered = lax.all_gather(density_factor, "col", axis=0, tiled=True)
    hits = (
        in_group[:, :, None] == jnp.arange(group_blocks, dtype=jnp.int32)[None, None, :]
    ).astype(jnp.float32)
    mixing = jnp.einsum("bkt,bkn->btn", kind_float, hits).astype(jnp.bfloat16)
    flat_blocks = gathered.reshape(group_blocks, block_rows * rank_cols)
    summed = jnp.einsum("btn,nm->btm", mixing, flat_blocks, preferred_element_type=jnp.float32)
    summed = summed.reshape(blocks, kinds, block_rows, rank_cols).astype(jnp.bfloat16)
    coupled = jnp.einsum(
        "tij,btjr->bir", coupling_blocks, summed, preferred_element_type=jnp.float32
    )
    own_rows = density_factor.reshape(blocks, block_rows, rank_cols)
    bath_pick = bath_blocks[bath_pattern]
    bathed = jnp.einsum(
        "bij,bjr->bir", bath_pick, own_rows, preferred_element_type=jnp.float32
    ).astype(jnp.bfloat16)
    factor_wide = own_rows.astype(jnp.float32)
    energy = onsite.reshape(blocks, block_rows, 1)
    moved = (factor_wide - time_step * (energy * factor_wide + coupled)).astype(jnp.bfloat16)
    stacked = jnp.concatenate([moved, bathed], axis=2).reshape(blocks * block_rows, 2 * rank_cols)
    local_gram = lax.dot_general(
        stacked, stacked, (((0,), (0,)), ((), ())), preferred_element_type=jnp.float32
    )
    gram_sum = lax.psum(local_gram, ("row", "col"))
    rotation = orthonormal_steps(gram_sum, rank_cols).astype(jnp.bfloat16)
    return jnp.dot(stacked, rotation, preferred_element_type=jnp.float32).astype(jnp.bfloat16)


def solution(mesh):
    placed = (
        P(("row", "col"), None),
        P(("row", "col")),
        P(("row", "col"), None),
        P(("row", "col")),
        P(("row", "col"), None),
        P(),
        P(("row", "col")),
        P(),
    )
    return jax.shard_map(
        shards, mesh=mesh, in_specs=placed, out_specs=P(("row", "col"), None), check_vma=False
    )
```

profile of v0, /device:TPU:1, one launch (start us, length us, event | category | flops | bytes accessed | tf_op | source)
XLA Modules:
  0.0 618.0 jit_solution(14788270948122039171)
XLA Ops:
  8.0 3.9 copy.12
  12.0 2.9 gather_fusion
  14.9 4.2 convolution_convert_fusion.1
  19.1 190.8 %all-gather.2.cloned.1.call-done = bf16[65536,256]{1,0:T(8,128)(2,1)} async-done(((bf16[4096,256]{1,0:T(8,128)(2,1)}), bf16[65536,256]{1,0:T(8,128)(2,1)}) %all-gather.2.cloned.1.call-update) | async-done | bytes 33554448 | tf_op jit(solution)/shard_map/all_gather | solution.py:45
  210.0 33.2 %reshape.54 = bf16[128,131072]{1,0:T(8,128)(2,1)} reshape(bf16[65536,256]{1,0:T(8,128)(2,1)} %all-gather.2.cloned.1.call-done) | data formatting | bytes 67108864 | tf_op jit(solution)/shard_map/reshape | solution.py:50
  243.2 23.1 %copy.24 = bf16[16,8,512,256]{3,2,1,0:T(8,128)(2,1)} copy(bf16[16,8,512,256]{3,1,2,0:T(8,128)(2,1)} %bitcast.98) | data formatting | bytes 67108864
  266.2 36.0 %fusion = bf16[8,4,512,256]{3,1,2,0:T(4,128)(2,1)} fusion(bf16[512,256,128,1]{1,0,2,3:T(8,128)(2,1)} %bitcast.99, s32[8,8]{1,0:T(8,128)S(1)} %broadcast_subtract_fusion, s32[8,8]{1,0:T(8,128)S(1)} %copy-done.5, pred[8,8]{1,0:T(8,128)(4,1)S(1)} %iota_compare_fusion.9), kind=kOutput, calls=%fused_computation.5 | convolution fusion | flops 1073820160 | bytes 41943616 | tf_op jit(solution)/shard_map/btn,nm->btm/dot_general | solution.py:51
  302.3 13.8 %copy.20 = bf16[8,4,512,256]{2,3,1,0:T(8,128)(2,1)} copy(bf16[8,4,512,256]{3,1,2,0:T(4,128)(2,1)} %fusion) | data formatting | bytes 16777216 | tf_op jit(solution)/shard_map/btn,nm->btm/dot_general | solution.py:51
  316.1 9.6 %fusion.6 = bf16[8,512,256]{1,2,0:T(8,128)(2,1)S(1)} fusion(bf16[8,512,256]{1,2,0:T(8,128)(2,1)} %copy.12, bf16[8,4,512,256]{2,3,1,0:T(8,128)(2,1)} %copy.20, bf16[4,512,512]{2,1,0:T(8,128)(2,1)} %param.16, f32[8,512]{1,0:T(8,128)S(1)} %mul.19), kind=kOutput, calls=%fused_computation.14 | convolution fusion | flops 4301258752 | bytes 14696448 | tf_op jit(solution)/shard_map/tij,btjr->bir/dot_general | solution.py:53
  325.7 1.3 copy-done.3
  327.0 3.3 convolution_bitcast_fusion
  330.3 3.8 pad_maximum_fusion
  334.2 6.5 %copy.14 = bf16[8,512,512]{2,1,0:T(8,128)(2,1)} copy(bf16[8,512,512]{1,2,0:T(8,128)(2,1)} %pad_maximum_fusion) | data formatting | bytes 8388608 | tf_op jit(solution)/shard_map/concatenate | solution.py:64
  340.6 136.9 %all-reduce.3.cloned.1.call-done = f32[512,512]{1,0:T(8,128)} async-done(((f32[512,512]{1,0:T(8,128)}), f32[512,512]{1,0:T(8,128)}) %all-reduce.3.cloned.1.call-update) | async-done | bytes 1048592 | tf_op jit(solution)/shard_map/psum | solution.py:68
  477.5 1.9 fusion.15
  479.4 1.0 fusion.49
  480.7 11.7 %cholesky.130 = f32[128,128]{1,0:T(8,128)S(1)} custom-call(f32[128,128]{1,0:T(8,128)S(1)} %cholesky.194), custom_call_target="Cholesky" | custom-call | tf_op jit(solution)/shard_map/jit(cholesky)/cholesky | solution.py:15
  492.4 9.8 %custom-call.13 = f32[1,128,128]{1,2,0:T(8,128)S(1)} custom-call(f32[1,128,128]{2,1,0:T(8,128)S(1)} %get-tuple-element.50), custom_call_target="InvertDiagBlocksLowerTriangular" | custom-call | tf_op jit(solution)/shard_map/jit(cholesky)/cholesky | solution.py:15
  502.7 11.7 %cholesky.147 = f32[128,128]{1,0:T(8,128)S(1)} custom-call(f32[128,128]{1,0:T(8,128)S(1)} %convolution_subtract_fusion.3), custom_call_target="Cholesky" | custom-call | tf_op jit(solution)/shard_map/jit(cholesky)/cholesky | solution.py:15
  516.6 4.0 while.4
  517.2 1.4 bitcast_dynamic-update-slice_fusion.4
  519.2 1.4 bitcast_dynamic-update-slice_fusion.4
  520.6 20.1 %custom-call.14 = f32[2,128,128]{1,2,0:T(8,128)S(1)} custom-call(f32[2,128,128]{2,1,0:T(8,128)S(1)} %get-tuple-element.21), custom_call_target="InvertDiagBlocksLowerTriangular" | custom-call | tf_op jit(solution)/shard_map/triangular_solve/custom-call.0 | solution.py:16
  543.1 1.0 fusion.50
  544.3 11.7 %cholesky.164 = f32[128,128]{1,0:T(8,128)S(1)} custom-call(f32[128,128]{1,0:T(8,128)S(1)} %cholesky.197), custom_call_target="Cholesky" | custom-call | tf_op jit(solution)/shard_map/jit(cholesky)/cholesky | solution.py:15
  556.7 9.8 %custom-call.15 = f32[1,128,128]{1,2,0:T(8,128)S(1)} custom-call(f32[1,128,128]{2,1,0:T(8,128)S(1)} %get-tuple-element.46), custom_call_target="InvertDiagBlocksLowerTriangular" | custom-call | tf_op jit(solution)/shard_map/jit(cholesky)/cholesky | solution.py:15
  567.1 11.9 %cholesky.181 = f32[128,128]{1,0:T(8,128)S(1)} custom-call(f32[128,128]{1,0:T(8,128)S(1)} %convolution_subtract_fusion.2), custom_call_target="Cholesky" | custom-call | tf_op jit(solution)/shard_map/jit(cholesky)/cholesky | solution.py:15
  580.9 3.9 while.5
  581.5 1.4 bitcast_dynamic-update-slice_fusion.5
  583.5 1.4 bitcast_dynamic-update-slice_fusion.5
  584.9 19.7 %custom-call.16 = f32[2,128,128]{1,2,0:T(8,128)S(1)} custom-call(f32[2,128,128]{2,1,0:T(8,128)S(1)} %get-tuple-element.22), custom_call_target="InvertDiagBlocksLowerTriangular" | custom-call | tf_op jit(solution)/shard_map/triangular_solve/custom-call.0 | solution.py:16
  606.0 4.9 convolution_convert_fusion
  (64 shorter events, 11.4 us)
Async XLA Ops:
  6.5 5.4 copy-start
  6.5 5.4 copy-start.6
  6.5 203.4 %all-gather.2.cloned.1.call-start = ((), (), s32[]{:S(2)}) async-start(), calls=%async_computation | async-start | bytes 35651584 | tf_op jit(solution)/shard_map/all_gather | solution.py:45
  7.3 470.3 %all-reduce.3.cloned.1.call-start = ((), (), s32[]{:S(2)}) async-start(), calls=%async_computation.1 | async-start | bytes 2097152 | tf_op jit(solution)/shard_map/psum | solution.py:68
  12.0 2.9 copy-start.7
  12.0 3.0 copy-start.4
  243.2 23.1 %copy-start.5 = (s32[8,8]{1,0:T(8,128)S(1)}, s32[8,8]{1,0:T(8,128)}, u32[]{:S(2)}) copy-start(s32[8,8]{1,0:T(8,128)} %param.15) | copy-start | bytes 772
  325.6 1.3 copy-start.3
  477.5 64.6 %copy-start.2 = (f32[512,512]{1,0:T(8,128)S(1)}, f32[512,512]{1,0:T(8,128)}, u32[]{:S(2)}) copy-start(f32[512,512]{1,0:T(8,128)} %all-reduce.3.cloned.1.call-done) | copy-start | bytes 3145732
  606.0 5.0 copy-start.1
Sparse Core Ops, SparseCore 0:
  9.5 200.4 all-gather.1
  330.4 147.0 all-reduce.2
where the time goes:
time: 623 us; the launch traced here: 618 us
  waiting for transfers between devices  328 us (53%)
  other arithmetic  113 us (18%)
  local copies, waits for them, and re-layouts  93.6 us (15%)
  matrix products  66.8 us (11%)
  between operations  16.5 us (3%)
    all_gather x1, waiting for transfers between devices, shards(): gathered = lax.all_gather(density_factor, 'col', axis=0, tiled=True)  191 us
    psum x1, waiting for transfers between devices, shards(): gram_sum = lax.psum(local_gram, ('row', 'col'))  137 us
    another operation x13, other arithmetic, orthonormal_steps(): factor = jnp.linalg.cholesky(inner)  68.8 us
    another operation x5, other arithmetic, orthonormal_steps(): lax.linalg.triangular_solve(factor, image, left_side=False, lower=True, t...  39.8 us
    dot_general x1, matrix products, shards(): jnp.einsum('btn,nm->btm', mixing, flat_blocks, preferred_element_type=jnp...  36 us
    reshape x1, local copies, waits for them, and re-layouts, shards(): flat_blocks = gathered.reshape(group_blocks, block_rows * rank_cols)  33.2 us
    unnamed x17, local copies, waits for them, and re-layouts  24.4 us
    dot_general x1, local copies, waits for them, and re-layouts, shards(): jnp.einsum('btn,nm->btm', mixing, flat_blocks, preferred_element_type=jnp...  13.8 us
  transfers between devices with their start and end apart: 2, of which 2 were waited for; matrix products, arithmetic and copies ran while one was open for 4% of the time, Pallas kernels for 0%

commit v1 on v0

--- a/solution.py
+++ b/solution.py
@@ -42,7 +42,8 @@
         coupling_type[:, :, None] == jnp.arange(kinds, dtype=jnp.int32)[None, None, :]
     ) & slot_live[:, :, None]
     kind_float = kind_match.astype(jnp.float32)
-    gathered = lax.all_gather(density_factor, "col", axis=0, tiled=True)
+    repeated = jnp.stack([density_factor] * lax.axis_size("col"))
+    gathered = jnp.concatenate(lax.all_to_all(repeated, "col", 0, 0), axis=0)
     hits = (
         in_group[:, :, None] == jnp.arange(group_blocks, dtype=jnp.int32)[None, None, :]
     ).astype(jnp.float32)

time: 623 us -> 1070 us (1.72)
  waiting for transfers between devices: 328 us -> 752 us
  local copies, waits for them, and re-layouts: 93.6 us -> 105 us
    all_to_all x0 -> x1, waiting for transfers between devices: none -> 609 us  [shards(): gathered = jnp.concatenate(lax.all_to_all(repeated, 'col', 0, 0), axis=0)]
    all_gather x1 -> x0, waiting for transfers between devices: 191 us -> none  [shards(): gathered = lax.all_gather(density_factor, 'col', axis=0, tiled=True)]
    another operation x0 -> x2, local copies, waits for them, and re-layouts: none -> 45.4 us  [the longest x1 33.2 us: shards(): flat_blocks = gathered.reshape(group_blocks, block_rows * rank_cols)]
    reshape x1 -> x0, local copies, waits for them, and re-layouts: 33.2 us -> none  [shards(): flat_blocks = gathered.reshape(group_blocks, block_rows * rank_cols)]
    unnamed x17 -> x19, local copies, waits for them, and re-layouts: 24.4 us -> 24.4 us
  transfers between devices with their start and end apart: 2 -> 2, of which waited for: 2 -> 2; matrix products, arithmetic and copies ran while one was open for 4% -> 2% of each run, Pallas kernels for 0% -> 0%
where the time goes in v1:
time: 1070 us; the launch traced here: 1060 us
  waiting for transfers between devices  752 us (70%)
  other arithmetic  113 us (11%)
  local copies, waits for them, and re-layouts  105 us (10%)
  matrix products  66.8 us (6%)
  between operations  16.5 us (2%)
    all_to_all x1, waiting for transfers between devices, shards(): gathered = jnp.concatenate(lax.all_to_all(repeated, 'col', 0, 0), axis=0)  609 us
    psum x1, waiting for transfers between devices, shards(): gram_sum = lax.psum(local_gram, ('row', 'col'))  143 us
    another operation x13, other arithmetic, orthonormal_steps(): factor = jnp.linalg.cholesky(inner)  68.7 us
    another operation x5, other arithmetic, orthonormal_steps(): lax.linalg.triangular_solve(factor, image, left_side=False, lower=True, t...  39.8 us
    dot_general x1, matrix products, shards(): jnp.einsum('btn,nm->btm', mixing, flat_blocks, preferred_element_type=jnp...  36 us
    another operation x1, local copies, waits for them, and re-layouts, shards(): flat_blocks = gathered.reshape(group_blocks, block_rows * rank_cols)  33.2 us
    unnamed x19, local copies, waits for them, and re-layouts  24.4 us
  transfers between devices with their start and end apart: 2, of which 2 were waited for; matrix products, arithmetic and copies ran while one was open for 2% of the time, Pallas kernels for 0%

profile of v1, /device:TPU:1, one launch (start us, length us, event | category | flops | bytes accessed | tf_op | source)
XLA Modules:
  0.0 1061.4 jit_solution(9854354641696324071)
XLA Ops:
  6.5 12.2 %stack.2 = bf16[16,4096,256]{2,1,0:T(8,128)(2,1)} broadcast(bf16[4096,256]{1,0:T(8,128)(2,1)} %param.11), dimensions={1,2} | broadcast | bytes 35651584 | tf_op jit(solution)/shard_map/stack | solution.py:45
  18.8 8.6 all-to-all-start
  27.5 3.9 copy.12
  31.5 2.8 gather_fusion
  34.4 4.2 convolution_convert_fusion.1
  38.5 608.6 %all-to-all-done = bf16[16,4096,256]{2,1,0:T(8,128)(2,1)} async-done(((bf16[16,4096,256]{2,1,0:T(8,128)(2,1)}), bf16[16,4096,256]{2,1,0:T(8,128)(2,1)}, u32[]{:S(2)}, u32[]{:S(2)}) %all-to-all-start) | async-done | bytes 33554464 | tf_op jit(solution)/shard_map/all_to_all | solution.py:46
  647.1 33.2 %reshape_reshape.3 = bf16[128,131072]{1,0:T(8,128)(2,1)} reshape(bf16[16,4096,256]{2,1,0:T(8,128)(2,1)} %all-to-all-done) | data formatting | bytes 67108864 | tf_op jit(solution)/shard_map/reshape;reshape | solution.py:51
  680.3 23.1 %copy.24 = bf16[16,8,512,256]{3,2,1,0:T(8,128)(2,1)} copy(bf16[16,8,512,256]{3,1,2,0:T(8,128)(2,1)} %bitcast.98) | data formatting | bytes 67108864
  703.4 36.0 %fusion = bf16[8,4,512,256]{3,1,2,0:T(4,128)(2,1)} fusion(bf16[512,256,128,1]{1,0,2,3:T(8,128)(2,1)} %bitcast.99, s32[8,8]{1,0:T(8,128)S(1)} %broadcast_subtract_fusion, s32[8,8]{1,0:T(8,128)S(1)} %copy-done.6, pred[8,8]{1,0:T(8,128)(4,1)S(1)} %iota_compare_fusion.9), kind=kOutput, calls=%fused_computation.5 | convolution fusion | flops 1073820160 | bytes 41943616 | tf_op jit(solution)/shard_map/btn,nm->btm/dot_general | solution.py:52
  739.4 13.8 %copy.20 = bf16[8,4,512,256]{2,3,1,0:T(8,128)(2,1)} copy(bf16[8,4,512,256]{3,1,2,0:T(4,128)(2,1)} %fusion) | data formatting | bytes 16777216 | tf_op jit(solution)/shard_map/btn,nm->btm/dot_general | solution.py:52
  753.2 9.6 fusion.6
  762.8 1.3 copy-done.3
  764.1 3.3 convolution_bitcast_fusion
  767.5 3.8 pad_maximum_fusion
  771.3 6.5 copy.14
  777.8 143.1 %all-reduce.3.cloned.1.call-done = f32[512,512]{1,0:T(8,128)} async-done(((f32[512,512]{1,0:T(8,128)}), f32[512,512]{1,0:T(8,128)}) %all-reduce.3.cloned.1.call-update) | async-done | bytes 1048592 | tf_op jit(solution)/shard_map/psum | solution.py:69
  920.9 1.9 fusion.15
  924.1 11.7 %cholesky.130 = f32[128,128]{1,0:T(8,128)S(1)} custom-call(f32[128,128]{1,0:T(8,128)S(1)} %cholesky.194), custom_call_target="Cholesky" | custom-call | tf_op jit(solution)/shard_map/jit(cholesky)/cholesky | solution.py:15
  935.8 9.8 custom-call.13
  946.2 11.7 %cholesky.147 = f32[128,128]{1,0:T(8,128)S(1)} custom-call(f32[128,128]{1,0:T(8,128)S(1)} %convolution_subtract_fusion.3), custom_call_target="Cholesky" | custom-call | tf_op jit(solution)/shard_map/jit(cholesky)/cholesky | solution.py:15
  960.0 4.0 while.4
  960.6 1.4 bitcast_dynamic-update-slice_fusion.4
  962.6 1.4 bitcast_dynamic-update-slice_fusion.4
  964.0 20.1 %custom-call.14 = f32[2,128,128]{1,2,0:T(8,128)S(1)} custom-call(f32[2,128,128]{2,1,0:T(8,128)S(1)} %get-tuple-element.21), custom_call_target="InvertDiagBlocksLowerTriangular" | custom-call | tf_op jit(solution)/shard_map/triangular_solve/custom-call.0 | solution.py:16
  987.8 11.7 %cholesky.164 = f32[128,128]{1,0:T(8,128)S(1)} custom-call(f32[128,128]{1,0:T(8,128)S(1)} %cholesky.197), custom_call_target="Cholesky" | custom-call | tf_op jit(solution)/shard_map/jit(cholesky)/cholesky | solution.py:15
  999.5 9.8 custom-call.15
  1009.8 11.9 %cholesky.181 = f32[128,128]{1,0:T(8,128)S(1)} custom-call(f32[128,128]{1,0:T(8,128)S(1)} %convolution_subtract_fusion.2), custom_call_target="Cholesky" | custom-call | tf_op jit(solution)/shard_map/jit(cholesky)/cholesky | solution.py:15
  1024.4 3.9 while.5
  1025.0 1.4 bitcast_dynamic-update-slice_fusion.5
  1026.9 1.4 bitcast_dynamic-update-slice_fusion.5
  1028.3 19.7 %custom-call.16 = f32[2,128,128]{1,2,0:T(8,128)S(1)} custom-call(f32[2,128,128]{2,1,0:T(8,128)S(1)} %get-tuple-element.22), custom_call_target="InvertDiagBlocksLowerTriangular" | custom-call | tf_op jit(solution)/shard_map/triangular_solve/custom-call.0 | solution.py:16
  1049.4 4.9 convolution_convert_fusion
  (66 shorter events, 12.1 us)
Async XLA Ops:
  6.5 24.9 %copy-start = (bf16[4,512,512]{2,1,0:T(8,128)(2,1)S(1)}, bf16[4,512,512]{2,1,0:T(8,128)(2,1)}, u32[]{:S(2)}) copy-start(bf16[4,512,512]{2,1,0:T(8,128)(2,1)} %param.18) | copy-start | bytes 6291460
  18.8 628.4 %all-to-all-start = ((bf16[16,4096,256]{2,1,0:T(8,128)(2,1)}), bf16[16,4096,256]{2,1,0:T(8,128)(2,1)}, u32[]{:S(2)}, u32[]{:S(2)}) async-start(bf16[16,4096,256]{2,1,0:T(8,128)(2,1)} %stack.2), calls=%async_computation | async-start | bytes 67108864 | tf_op jit(solution)/shard_map/all_to_all | solution.py:46
  27.4 4.0 copy-start.4
  27.4 4.0 copy-start.7
  27.4 893.5 %all-reduce.3.cloned.1.call-start = ((), (), s32[]{:S(2)}) async-start(), calls=%async_computation.1 | async-start | bytes 2097152 | tf_op jit(solution)/shard_map/psum | solution.py:69
  31.5 2.8 copy-start.8
  31.5 2.9 copy-start.5
  680.3 23.1 %copy-start.6 = (s32[8,8]{1,0:T(8,128)S(1)}, s32[8,8]{1,0:T(8,128)}, u32[]{:S(2)}) copy-start(s32[8,8]{1,0:T(8,128)} %param.15) | copy-start | bytes 772
  762.8 1.3 copy-start.3
  920.9 64.6 %copy-start.2 = (f32[512,512]{1,0:T(8,128)S(1)}, f32[512,512]{1,0:T(8,128)}, u32[]{:S(2)}) copy-start(f32[512,512]{1,0:T(8,128)} %all-reduce.3.cloned.1.call-done) | copy-start | bytes 3145732
  1049.4 5.0 copy-start.1
Sparse Core Ops, SparseCore 0:
  767.6 153.2 all-reduce.2
